TPU v7x, 32 devices: a whole 2x2x4 slice. The times are simulated.
32 devices in a mesh: expert: 4 (over y, core), fsdp: 8 (over z, x).
Axes of the slice: x: 2, y: 2, z: 4, core: 2. Of those that a mesh axis runs over, the one named last changes fastest.
Arguments:
- layer_input: bfloat16 [8192, 2048], P(('expert', 'fsdp')), may hold values from -6 to 6
- expert_ids: int32 [8192, 8], P(('expert', 'fsdp')), may hold values from 0 to 15, as said below
- slot_ids: int32 [8192, 8], P(('expert', 'fsdp')), may hold values from 0 to 255, as said below
- attn_gain: float32 [2048], replicated, may hold values from 0.25 to 1.75
- qkv_weight: bfloat16 [2048, 6144], P('fsdp'), may hold values from -0.125 to 0.125
- query_gain: float32 [128], replicated, may hold values from 0.25 to 1.75
- key_gain: float32 [128], replicated, may hold values from 0.25 to 1.75
- out_weight: bfloat16 [2048, 2048], P('fsdp'), may hold values from -1 to 1
- ffn_gain: float32 [2048], replicated, may hold values from 0.25 to 1.75
- router_weight: bfloat16 [2048, 16], P('fsdp'), may hold values from -0.0625 to 0.0625
- gate_up_weight: bfloat16 [16, 2048, 2048], P('expert', 'fsdp'), may hold values from -0.125 to 0.125
- down_weight: bfloat16 [16, 1024, 2048], P('expert', 'fsdp'), may hold values from -0.75 to 0.75
- cotangent: bfloat16 [8192, 2048], P(('expert', 'fsdp')), may hold values from -6 to 6
Outputs:
- mixed_out: bfloat16 [8192, 2048], P(('expert', 'fsdp'))
- input_grad: float32 [8192, 2048], P(('expert', 'fsdp'))
- attn_gain_grad: float32 [2048], replicated
- qkv_weight_grad: float32 [2048, 6144], P('fsdp')
- query_gain_grad: float32 [128], replicated
- key_gain_grad: float32 [128], replicated
- out_weight_grad: float32 [2048, 2048], P('fsdp')
- ffn_gain_grad: float32 [2048], replicated
- router_weight_grad: float32 [2048, 16], P('fsdp')
- gate_up_grad: float32 [16, 2048, 2048], P('expert', 'fsdp')
- down_grad: float32 [16, 1024, 2048], P('expert', 'fsdp')
Inputs may be any that keep to these rules, and one draw needn't show every extreme that they name: `expert_ids`: each row names 8 different experts. Among the 256 rows of one device no expert is named more than 256 times; in every device's rows one expert is named exactly 256 times. `slot_ids`: among the rows of one device, the routes to one expert have different slots.
All inputs are finite; a program needn't handle non-finite values.
Results may differ from a plain program's by a relative error of at most 0.022.
Values may be sent and summed in bfloat16 or wider, within the bound.
No kernel may reach another device: no remote copies, remote signals or barrier semaphores. Data moves between devices by JAX's collectives and lax.ppermute only.
A program may use at most 384 MiB of HBM per device.

v0:
```python
import jax
import jax.numpy as jnp
from jax import lax
from jax.sharding import PartitionSpec as P

EPSILON = 1e-06
ROPE_BASE = 50000.0


def normalize(values):
    factor = lax.rsqrt(jnp.mean(values * values, -1, keepdims=True) + EPSILON)
    return (values * factor, factor)


def norm_back(grad_unit, unit_val, factor):
    return factor * (grad_unit - unit_val * jnp.mean(grad_unit * unit_val, -1, keepdims=True))


def tables(length, head_size):
    half_size = head_size // 2
    frequency = ROPE_BASE ** (-(jnp.arange(half_size, dtype=jnp.float32) * 2.0 / head_size))
    angles = jnp.arange(length, dtype=jnp.float32)[:, None] * frequency[None, :]
    angles = jnp.concatenate([angles, angles], 1)
    return (jnp.cos(angles)[:, None, :], jnp.sin(angles)[:, None, :])


def rotate(values, cos_table, sine_table):
    half_size = values.shape[-1] // 2
    turned = jnp.concatenate([-values[..., half_size:], values[..., :half_size]], -1)
    return values * cos_table + turned * sine_table


def rotate_back(gradient, cos_table, sine_table):
    half_size = gradient.shape[-1] // 2
    turned_grad = gradient * sine_table
    return gradient * cos_table + jnp.concatenate(
        [turned_grad[..., half_size:], -turned_grad[..., :half_size]], -1
    )


def local(
    layer_input,
    expert_ids,
    slot_ids,
    attn_gain,
    qkv_weight,
    query_gain,
    key_gain,
    out_weight,
    ffn_gain,
    router_weight,
    gate_up_weight,
    down_weight,
    cotangent,
):
    tokens, model_width = layer_input.shape
    top_count = expert_ids.shape[1]
    head_size = query_gain.shape[0]
    head_count = model_width // head_size
    experts = router_weight.shape[1]
    hidden = gate_up_weight.shape[2] // 2
    capacity = 2 * tokens * top_count // experts
    score_scale = head_size ** (-0.5)
    source = layer_input.astype(jnp.float32)
    unit_one, factor_one = normalize(source)
    normed = (unit_one * attn_gain).astype(jnp.bfloat16)
    qkv_full, out_full, router_full = (
        lax.all_gather(qkv_weight, "fsdp", axis=0, tiled=True),
        lax.all_gather(out_weight, "fsdp", axis=0, tiled=True),
        lax.all_gather(router_weight, "fsdp", axis=0, tiled=True),
    )
    projected = jnp.dot(normed, qkv_full, preferred_element_type=jnp.float32)
    queries = projected[:, :model_width].reshape(tokens, head_count, head_size)
    keys_raw = projected[:, model_width : 2 * model_width].reshape(tokens, head_count, head_size)
    values_raw = projected[:, 2 * model_width :].reshape(tokens, head_count, head_size)
    unit_query, factor_query = normalize(queries)
    unit_key, factor_key = normalize(keys_raw)
    cos_table, sine_table = tables(tokens, head_size)
    query_rot = rotate(unit_query * query_gain, cos_table, sine_table).astype(jnp.bfloat16)
    key_rot = rotate(unit_key * key_gain, cos_table, sine_table).astype(jnp.bfloat16)
    value_low = values_raw.astype(jnp.bfloat16)
    scores = (
        jnp.einsum("qhd,khd->hqk", query_rot, key_rot, preferred_element_type=jnp.float32)
        * score_scale
    )
    top_score = jnp.max(scores, -1, keepdims=True)
    weights_raw = jnp.exp(scores - top_score)
    totals = jnp.sum(weights_raw, -1, keepdims=True)
    log_total = top_score + jnp.log(totals)
    prob_low = (weights_raw / totals).astype(jnp.bfloat16)
    mixed_heads = jnp.einsum(
        "hqk,khd->qhd", prob_low, value_low, preferred_element_type=jnp.float32
    )
    mixed_low = mixed_heads.reshape(tokens, model_width).astype(jnp.bfloat16)
    residual = source + jnp.dot(mixed_low, out_full, preferred_element_type=jnp.float32)
    unit_two, factor_two = normalize(residual)
    normed_two = (unit_two * ffn_gain).astype(jnp.bfloat16)
    logits = jnp.dot(normed_two, router_full, preferred_element_type=jnp.float32)
    onehot = (expert_ids[:, :, None] == jnp.arange(experts, dtype=jnp.int32)[None, None, :]).astype(
        jnp.float32
    )
    chosen = jnp.sum(onehot * logits[:, None, :], -1)
    gate_probs = jax.nn.softmax(chosen, -1)
    slot_index = (expert_ids * capacity + slot_ids).reshape(-1)
    copies = jnp.broadcast_to(normed_two[:, None, :], (tokens, top_count, model_width)).reshape(
        tokens * top_count, model_width
    )
    outgoing = jnp.zeros((experts * capacity, model_width), jnp.bfloat16).at[slot_index].set(copies)
    arrived = lax.all_to_all(
        outgoing.reshape(experts, capacity, model_width),
        "expert",
        split_axis=0,
        concat_axis=1,
        tiled=True,
    )
    gate_up_full, down_full = (
        lax.all_gather(gate_up_weight, "fsdp", axis=1, tiled=True),
        lax.all_gather(down_weight, "fsdp", axis=1, tiled=True),
    )
    gate_up_val = jnp.einsum(
        "erd,edf->erf", arrived, gate_up_full, preferred_element_type=jnp.float32
    )
    gate_part = gate_up_val[..., :hidden]
    up_part = gate_up_val[..., hidden:]
    sigmoid_gate = jax.nn.sigmoid(gate_part)
    activated = (gate_part * sigmoid_gate * up_part).astype(jnp.bfloat16)
    expert_out = jnp.einsum(
        "erf,efd->erd", activated, down_full, preferred_element_type=jnp.float32
    ).astype(jnp.bfloat16)
    returned = lax.all_to_all(
        expert_out, "expert", split_axis=1, concat_axis=0, tiled=True
    ).reshape(experts * capacity, model_width)
    picked = returned[slot_index].reshape(tokens, top_count, model_width).astype(jnp.float32)
    moe_sum = jnp.sum(gate_probs[:, :, None] * picked, 1)
    mixed_out = (residual + moe_sum).astype(jnp.bfloat16)
    upstream = cotangent.astype(jnp.float32)
    gate_grad = jnp.sum(picked * upstream[:, None, :], -1)
    row_grad = (
        (gate_probs[:, :, None] * upstream[:, None, :])
        .astype(jnp.bfloat16)
        .reshape(tokens * top_count, model_width)
    )
    grad_out = (
        jnp.zeros((experts * capacity, model_width), jnp.bfloat16).at[slot_index].set(row_grad)
    )
    grad_arrived = lax.all_to_all(
        grad_out.reshape(experts, capacity, model_width),
        "expert",
        split_axis=0,
        concat_axis=1,
        tiled=True,
    )
    gate_up_back, down_back = (
        lax.all_gather(gate_up_weight, "fsdp", axis=1, tiled=True),
        lax.all_gather(down_weight, "fsdp", axis=1, tiled=True),
    )
    act_grad = jnp.einsum(
        "erd,efd->erf", grad_arrived, down_back, preferred_element_type=jnp.float32
    )
    down_grad_full = jnp.einsum(
        "erf,erd->efd", activated, grad_arrived, preferred_element_type=jnp.float32
    )
    gate_grad_part = act_grad * up_part * sigmoid_gate * (1.0 + gate_part * (1.0 - sigmoid_gate))
    up_grad_part = act_grad * gate_part * sigmoid_gate
    both_grad = jnp.concatenate([gate_grad_part, up_grad_part], -1).astype(jnp.bfloat16)
    gate_up_grad_full = jnp.einsum(
        "erd,erf->edf", arrived, both_grad, preferred_element_type=jnp.float32
    )
    input_rows = jnp.einsum(
        "erf,edf->erd", both_grad, gate_up_back, preferred_element_type=jnp.float32
    ).astype(jnp.bfloat16)
    rows_back = lax.all_to_all(
        input_rows, "expert", split_axis=1, concat_axis=0, tiled=True
    ).reshape(experts * capacity, model_width)
    gate_up_grad, down_grad = (
        lax.psum_scatter(
            gate_up_grad_full.astype(jnp.bfloat16), "fsdp", scatter_dimension=1, tiled=True
        ).astype(jnp.float32),
        lax.psum_scatter(
            down_grad_full.astype(jnp.bfloat16), "fsdp", scatter_dimension=1, tiled=True
        ).astype(jnp.float32),
    )
    mean_grad = jnp.sum(gate_probs * gate_grad, -1, keepdims=True)
    chosen_grad = gate_probs * (gate_grad - mean_grad)
    logit_grad = jnp.sum(onehot * chosen_grad[:, :, None], 1).astype(jnp.bfloat16)
    router_grad_full = jnp.dot(normed_two.T, logit_grad, preferred_element_type=jnp.float32)
    routed_back = jnp.sum(
        rows_back[slot_index].reshape(tokens, top_count, model_width).astype(jnp.float32), 1
    )
    normed_two_grad = routed_back + jnp.dot(
        logit_grad, router_full.T, preferred_element_type=jnp.float32
    )
    ffn_gain_part = jnp.sum(normed_two_grad * unit_two, 0)
    residual_grad = upstream + norm_back(normed_two_grad * ffn_gain, unit_two, factor_two)
    attn_grad_low = residual_grad.astype(jnp.bfloat16)
    out_grad_full = jnp.dot(mixed_low.T, attn_grad_low, preferred_element_type=jnp.float32)
    mixed_grad = jnp.dot(attn_grad_low, out_full.T, preferred_element_type=jnp.float32).astype(
        jnp.bfloat16
    )
    mixed_grad = mixed_grad.reshape(tokens, head_count, head_size)
    value_grad = jnp.einsum(
        "hqk,qhd->khd", prob_low, mixed_grad, preferred_element_type=jnp.float32
    )
    prob_grad = jnp.einsum(
        "qhd,khd->hqk", mixed_grad, value_low, preferred_element_type=jnp.float32
    )
    scores_again = (
        jnp.einsum("qhd,khd->hqk", query_rot, key_rot, preferred_element_type=jnp.float32)
        * score_scale
    )
    prob_full = jnp.exp(scores_again - log_total)
    score_grad = (
        prob_full * (prob_grad - jnp.sum(prob_full * prob_grad, -1, keepdims=True))
    ).astype(jnp.bfloat16)
    query_grad = (
        jnp.einsum("hqk,khd->qhd", score_grad, key_rot, preferred_element_type=jnp.float32)
        * score_scale
    )
    key_grad = (
        jnp.einsum("hqk,qhd->khd", score_grad, query_rot, preferred_element_type=jnp.float32)
        * score_scale
    )
    query_grad = rotate_back(query_grad, cos_table, sine_table)
    key_grad = rotate_back(key_grad, cos_table, sine_table)
    query_gain_part = jnp.sum(query_grad * unit_query, (0, 1))
    key_gain_part = jnp.sum(key_grad * unit_key, (0, 1))
    query_pre = norm_back(query_grad * query_gain, unit_query, factor_query)
    key_pre = norm_back(key_grad * key_gain, unit_key, factor_key)
    qkv_grad_low = jnp.concatenate(
        [
            query_pre.reshape(tokens, model_width),
            key_pre.reshape(tokens, model_width),
            value_grad.reshape(tokens, model_width),
        ],
        1,
    ).astype(jnp.bfloat16)
    qkv_grad_full = jnp.dot(normed.T, qkv_grad_low, preferred_element_type=jnp.float32)
    normed_grad = jnp.dot(qkv_grad_low, qkv_full.T, preferred_element_type=jnp.float32)
    attn_gain_part = jnp.sum(normed_grad * unit_one, 0)
    input_grad = residual_grad + norm_back(normed_grad * attn_gain, unit_one, factor_one)
    qkv_shard, out_shard, router_shard = (
        lax.psum_scatter(
            qkv_grad_full.astype(jnp.bfloat16), "fsdp", scatter_dimension=0, tiled=True
        ).astype(jnp.float32),
        lax.psum_scatter(
            out_grad_full.astype(jnp.bfloat16), "fsdp", scatter_dimension=0, tiled=True
        ).astype(jnp.float32),
        lax.psum_scatter(
            router_grad_full.astype(jnp.bfloat16), "fsdp", scatter_dimension=0, tiled=True
        ).astype(jnp.float32),
    )
    qkv_weight_grad, out_weight_grad, router_weight_grad = (
        lax.psum(qkv_shard.astype(jnp.bfloat16), "expert").astype(jnp.float32),
        lax.psum(out_shard.astype(jnp.bfloat16), "expert").astype(jnp.float32),
        lax.psum(router_shard.astype(jnp.bfloat16), "expert").astype(jnp.float32),
    )
    attn_gain_grad, query_gain_grad, key_gain_grad, ffn_gain_grad = lax.psum(
        (attn_gain_part, query_gain_part, key_gain_part, ffn_gain_part), ("expert", "fsdp")
    )
    return (
        mixed_out,
        input_grad,
        attn_gain_grad,
        qkv_weight_grad,
        query_gain_grad,
        key_gain_grad,
        out_weight_grad,
        ffn_gain_grad,
        router_weight_grad,
        gate_up_grad,
        down_grad,
    )


def solution(mesh):
    return jax.shard_map(
        local,
        mesh=mesh,
        in_specs=(
            P(("expert", "fsdp"), None),
            P(("expert", "fsdp"), None),
            P(("expert", "fsdp"), None),
            P(),
            P("fsdp", None),
            P(),
            P(),
            P("fsdp", None),
            P(),
            P("fsdp", None),
            P("expert", "fsdp", None),
            P("expert", "fsdp", None),
            P(("expert", "fsdp"), None),
        ),
        out_specs=(
            P(("expert", "fsdp"), None),
            P(("expert", "fsdp"), None),
            P(),
            P("fsdp", None),
            P(),
            P(),
            P("fsdp", None),
            P(),
            P("fsdp", None),
            P("expert", "fsdp", None),
            P("expert", "fsdp", None),
        ),
        check_vma=False,
    )
```

profile of v0, /device:TPU:0, one launch (start us, length us, event | category | flops | bytes accessed | tf_op | source)
XLA Modules:
  0.0 3566.4 jit_solution(18210329636455333657)
XLA Ops:
  9.7 1.5 convert_element_type.132
  11.3 67.9 %all_gather.19 = bf16[2048,16]{0,1:T(8,128)(2,1)S(1)} all-gather(bf16[256,16]{0,1:T(8,128)(2,1)S(1)} %copy-done.66), channel_id=1, replica_groups=mesh['expert'=4,'fsdp'=8] {'fsdp'}, dimensions={0}, use_global_device_ids=true | all-gather | bytes 73728 | tf_op jit(solution)/shard_map/all_gather | solution.py:70
  80.8 413.0 %all-gather.5.cloned.1.call-done = bf16[2048,6144]{1,0:T(8,128)(2,1)} async-done(((bf16[256,6144]{1,0:T(8,128)(2,1)}), bf16[2048,6144]{1,0:T(8,128)(2,1)}) %all-gather.5.cloned.1.call-update) | async-done | bytes 25165840 | tf_op jit(solution)/shard_map/all_gather | solution.py:68
  493.8 11.7 fusion.38
  505.5 1.9 slice_bitcast_fusion
  507.4 1.4 copy-done.20
  508.8 1.7 copy.226
  510.5 1.9 copy.188
  512.5 3.6 multiply_reduce_fusion.9
  517.1 3.3 copy.225
  520.4 3.4 copy.186
  523.8 2.9 multiply_reduce_fusion.10
  527.8 2.2 multiply_multiply_fusion
  535.6 2.1 convolution_convert_fusion.9
  537.7 83.1 %all-gather.7.cloned.1.call-done = bf16[2048,2048]{1,0:T(8,128)(2,1)} async-done(((bf16[256,2048]{1,0:T(8,128)(2,1)}), bf16[2048,2048]{1,0:T(8,128)(2,1)}) %all-gather.7.cloned.1.call-update) | async-done | bytes 8388624 | tf_op jit(solution)/shard_map/all_gather | solution.py:69
  620.8 5.8 multiply_reduce_fusion.8
  629.6 22.2 scatter_custom_fusion.1
  651.8 7.0 all-to-all-start.2
  659.4 21.2 scatter_custom_fusion
  680.6 161.2 %all-to-all-done.2 = bf16[16,256,2048]{2,1,0:T(8,128)(2,1)} async-done(((bf16[16,256,2048]{2,1,0:T(8,128)(2,1)}), bf16[16,256,2048]{2,1,0:T(8,128)(2,1)}, u32[]{:S(2)}, u32[]{:S(2)}) %all-to-all-start.2) | async-done | bytes 16777248 | tf_op jit(solution)/shard_map/all_to_all | solution.py:146
  841.9 7.6 all-to-all-start
  849.5 14.2 copy.199
  863.7 168.8 %all-to-all-done = bf16[16,256,2048]{2,1,0:T(8,128)(2,1)} async-done(((bf16[16,256,2048]{2,1,0:T(8,128)(2,1)}), bf16[16,256,2048]{2,1,0:T(8,128)(2,1)}, u32[]{:S(2)}, u32[]{:S(2)}) %all-to-all-start) | async-done | bytes 16777248 | tf_op jit(solution)/shard_map/all_to_all | solution.py:109
  1032.5 14.2 copy.195
  1046.7 211.6 %all-gather.9.cloned.1.call-done = bf16[4,2048,2048]{2,1,0:T(8,128)(2,1)} async-done(((bf16[4,256,2048]{2,1,0:T(8,128)(2,1)}), bf16[4,2048,2048]{2,1,0:T(8,128)(2,1)}) %all-gather.9.cloned.1.call-update) | async-done | bytes 33554448 | tf_op jit(solution)/shard_map/all_gather | solution.py:117
  1258.3 43.2 %fusion.53 = f32[4,1024,2048]{2,1,0:T(8,128)} fusion(bf16[4,1024,2048]{2,1,0:T(8,128)(2,1)} %bitcast.118, bf16[4,2048,2048]{2,1,0:T(8,128)(2,1)} %all-gather.9.cloned.1.call-done), kind=kOutput, calls=%fused_computation.138 | convolution fusion | flops 34359738368 | bytes 83886080 | tf_op jit(solution)/shard_map/erd,edf->erf/dot_general | solution.py:120
  1301.5 186.5 %all-gather.11.cloned.1.call-done = bf16[4,1024,2048]{2,1,0:T(8,128)(2,1)} async-done(((bf16[4,128,2048]{2,1,0:T(8,128)(2,1)}), bf16[4,1024,2048]{2,1,0:T(8,128)(2,1)}) %all-gather.11.cloned.1.call-update) | async-done | bytes 16777232 | tf_op jit(solution)/shard_map/all_gather | solution.py:118
  1488.0 37.0 %multiply_convert_fusion.1 = (bf16[4,1024,1024]{2,1,0:T(8,128)(2,1)}, bf16[4,1024,1024]{2,1,0:T(8,128)(2,1)}, bf16[4,1024,1024]{2,1,0:T(8,128)(2,1)}) fusion(f32[4,1024,2048]{2,1,0:T(8,128)} %fusion.53, bf16[4,1024,2048]{2,1,0:T(8,128)(2,1)} %bitcast.120, bf16[4,1024,2048]{2,1,0:T(8,128)(2,1)} %all-gather.11.cloned.1.call-done), kind=kOutput, calls=%fused_computation.15 | convolution fusion | flops 17246978048 | bytes 92274688 | tf_op jit(solution)/shard_map/erd,efd->erf/dot_general | solution.py:157
  1525.0 27.2 convolution_convert_fusion.4
  1552.2 22.1 copy.196
  1574.3 7.1 all-to-all-start.1
  1581.4 43.4 %convolution_convert_fusion.2 = bf16[4,1024,2048]{2,1,0:T(8,128)(2,1)} fusion(bf16[4,2048,2048]{2,1,0:T(8,128)(2,1)} %all-gather.9.cloned.1.call-done, bf16[4,1024,1024]{2,1,0:T(8,128)(2,1)} %get-tuple-element.30, bf16[4,1024,1024]{2,1,0:T(8,128)(2,1)} %get-tuple-element.29), kind=kOutput, calls=%fused_computation.18 | convolution fusion | flops 34401681408 | bytes 67108864 | tf_op jit(solution)/shard_map/erf,edf->erd/dot_general | solution.py:169
  1624.8 22.1 copy.202
  1646.9 117.5 %all-to-all-done.1 = bf16[4,1024,2048]{2,0,1:T(4,128)(2,1)} async-done(((bf16[4,1024,2048]{2,0,1:T(4,128)(2,1)}), bf16[4,1024,2048]{2,0,1:T(4,128)(2,1)}, u32[]{:S(2)}, u32[]{:S(2)}) %all-to-all-start.1) | async-done | bytes 16777248 | tf_op jit(solution)/shard_map/all_to_all | solution.py:130
  1764.5 7.2 all-to-all-start.3
  1771.8 18.6 copy.197
  1790.4 24.4 gather_fusion
  1814.8 9.5 fusion.1
  1824.5 130.2 %all-to-all-done.3 = bf16[4,1024,2048]{2,0,1:T(4,128)(2,1)} async-done(((bf16[4,1024,2048]{2,0,1:T(4,128)(2,1)}), bf16[4,1024,2048]{2,0,1:T(4,128)(2,1)}, u32[]{:S(2)}, u32[]{:S(2)}) %all-to-all-start.3) | async-done | bytes 16777248 | tf_op jit(solution)/shard_map/all_to_all | solution.py:172
  1954.7 18.6 copy.203
  1973.3 24.6 gather_fusion.1
  1998.0 11.4 convert_reduce_fusion
  2009.5 3.1 multiply_reduce_fusion.2
  2012.6 1.8 multiply_add_fusion
  2015.7 5.6 convolution_convert_fusion.5
  2022.9 6.1 convolution_convert_fusion.6
  2029.5 4.1 multiply_reduce_fusion
  2039.1 3.0 multiply_reduce_fusion.4
  2045.1 14.6 convolution_convert_fusion.1
  2061.9 27.1 convolution_convert_fusion.3
  2089.1 78.6 %reduce-scatter.8.cloned.1.call-done = bf16[256,2048]{1,0:T(8,128)(2,1)} async-done(((bf16[2048,2048]{1,0:T(8,128)(2,1)}), bf16[256,2048]{1,0:T(8,128)(2,1)}) %reduce-scatter.8.cloned.1.call-update) | async-done | bytes 1048592 | tf_op jit(solution)/shard_map/reduce_scatter | solution.py:245
  2167.7 407.0 %reduce-scatter.6.cloned.1.call-done = bf16[256,6144]{1,0:T(8,128)(2,1)} async-done(((bf16[2048,6144]{1,0:T(8,128)(2,1)}), bf16[256,6144]{1,0:T(8,128)(2,1)}) %reduce-scatter.6.cloned.1.call-update) | async-done | bytes 3145744 | tf_op jit(solution)/shard_map/reduce_scatter | solution.py:242
  2574.8 43.8 %convolution_convert_fusion = bf16[4,2048,2048]{2,1,0:T(8,128)(2,1)} fusion(bf16[4,1024,2048]{2,1,0:T(8,128)(2,1)} %bitcast.119, bf16[4,1024,1024]{2,1,0:T(8,128)(2,1)} %get-tuple-element.30, bf16[4,1024,1024]{2,1,0:T(8,128)(2,1)} %get-tuple-element.29), kind=kOutput, calls=%fused_computation.4 | convolution fusion | flops 34410070016 | bytes 67108864 | tf_op jit(solution)/shard_map/erd,erf->edf/dot_general | solution.py:166
  2618.7 14.2 fusion.22
  2633.0 43.8 %all-reduce = (f32[2048]{0:T(1024)}, f32[128]{0:T(128)}, f32[128]{0:T(128)}, f32[2048]{0:T(1024)}) all-reduce(f32[2048]{0:T(1024)S(1)} %get-tuple-element.19, f32[128]{0:T(128)S(1)} %copy-done.71, f32[128]{0:T(128)S(1)} %copy-done.72, f32[2048]{0:T(1024)S(1)} %copy-done.56), channel_id=1, replica_groups=mesh['expert'=4,'fsdp'=8] {'expert','fsdp'}, use_global_device_ids=true, to_apply=%region_22.0 | all-reduce | flops 4352 | bytes 34816 | tf_op jit(solution)/shard_map/psum | solution.py:257
  2676.8 3.5 fusion.21
  2680.2 6.7 psum.55
  2687.6 230.5 %reduce-scatter.14.cloned.1.call-done = bf16[4,128,2048]{2,1,0:T(8,128)(2,1)} async-done(((bf16[4,1024,2048]{2,1,0:T(8,128)(2,1)}), bf16[4,128,2048]{2,1,0:T(8,128)(2,1)}) %reduce-scatter.14.cloned.1.call-update) | async-done | bytes 2097168 | tf_op jit(solution)/shard_map/reduce_scatter | solution.py:179
  2918.1 4.1 convert_element_type.150
  2922.2 83.0 %all-reduce.4.cloned.1.call-done = (bf16[256,6144]{1,0:T(8,128)(2,1)}, bf16[256,2048]{1,0:T(8,128)(2,1)}) async-done(((bf16[256,6144]{1,0:T(8,128)(2,1)}, bf16[256,2048]{1,0:T(8,128)(2,1)}), (bf16[256,6144]{1,0:T(8,128)(2,1)}, bf16[256,2048]{1,0:T(8,128)(2,1)})) %all-reduce.4.cloned.1.call-update) | async-done | bytes 4194320 | tf_op jit(solution)/shard_map/psum | solution.py:253
  3005.3 2.9 convert_element_type.144
  3008.2 3.4 convert_element_type.142
  3011.6 541.0 %reduce-scatter.12.cloned.1.call-done = bf16[4,256,2048]{2,1,0:T(8,128)(2,1)} async-done(((bf16[4,2048,2048]{2,1,0:T(8,128)(2,1)}), bf16[4,256,2048]{2,1,0:T(8,128)(2,1)}) %reduce-scatter.12.cloned.1.call-update) | async-done | bytes 4194320 | tf_op jit(solution)/shard_map/reduce_scatter | solution.py:176
  3552.6 6.7 convert_element_type.148
  (215 shorter events, 29.8 us)
Async XLA Ops:
  7.2 486.6 %all-gather.5.cloned.1.call-start = ((), (), s32[]{:S(2)}) async-start(), calls=%async_computation.9 | async-start | bytes 28311552 | tf_op jit(solution)/shard_map/all_gather | solution.py:68
  7.2 2.2 copy-start.54
  7.2 2.2 copy-start.65
  7.2 2.5 copy-start.26
  7.9 3.4 copy-start.66
  7.9 612.9 %all-gather.7.cloned.1.call-start = ((), (), s32[]{:S(2)}) async-start(), calls=%async_computation.10 | async-start | bytes 9437184 | tf_op jit(solution)/shard_map/all_gather | solution.py:69
  8.7 71.8 %copy-start.14 = (bf16[256,2048]{1,0:T(8,128)(2,1)S(1)}, bf16[256,2048]{1,0:T(8,128)(2,1)}, u32[]{:S(2)}) copy-start(bf16[256,2048]{1,0:T(8,128)(2,1)} %param.13) | copy-start | bytes 3145732
  8.7 485.1 %copy-start.34 = (f32[2048]{0:T(1024)S(1)}, f32[2048]{0:T(1024)}, u32[]{:S(2)}) copy-start(f32[2048]{0:T(1024)} %param.16) | copy-start | bytes 24580
  8.7 1249.6 %all-gather.9.cloned.1.call-start = ((), (), s32[]{:S(2)}) async-start(), calls=%async_computation.11 | async-start | bytes 37748736 | tf_op jit(solution)/shard_map/all_gather | solution.py:117
  79.2 549.1 %copy-start.36 = (bf16[2048,16]{0,1:T(8,128)(2,1)}, bf16[2048,16]{0,1:T(8,128)(2,1)S(1)}, u32[]{:S(2)}) copy-start(bf16[2048,16]{0,1:T(8,128)(2,1)S(1)} %all_gather.19) | copy-start | bytes 196612
  80.8 424.7 %copy-start.50 = (f32[256]{0:T(256)}, f32[256]{0:T(256)S(1)}, u32[]{:S(2)}) copy-start(f32[256]{0:T(256)S(1)} %add_rsqrt_fusion.3) | copy-start | bytes 3076
  80.8 578.6 %copy-start.57 = (s32[2048,1]{0,1:T(1,128)}, s32[2048,1]{0,1:T(1,128)S(1)}, u32[]{:S(2)}) copy-start(s32[2048,1]{0,1:T(1,128)S(1)} %compare_select_fusion) | copy-start | bytes 24580
  505.5 3.3 copy-start.20
  512.5 15.3 copy-start.4
  520.4 7.3 copy-start.67
  520.4 7.4 copy-start.69
  527.7 2.3 copy-start.44
  527.7 2.2 copy-start.46
  537.7 83.1 %copy-start.18 = (bf16[16,128,256]{2,1,0:T(8,128)(2,1)}, bf16[16,128,256]{2,1,0:T(8,128)(2,1)S(1)}, u32[]{:S(2)}) copy-start(bf16[16,128,256]{2,1,0:T(8,128)(2,1)S(1)} %convolution_convert_fusion.9) | copy-start | bytes 3145732
  620.8 7.2 copy-start.52
  626.7 2.9 copy-start.10
  626.7 25.1 copy-start.61
  628.3 31.2 copy-start.16
  629.3 22.5 copy-start.63
  629.5 22.3 copy-start.32
  651.8 190.1 %all-to-all-start.2 = ((bf16[16,256,2048]{2,1,0:T(8,128)(2,1)}), bf16[16,256,2048]{2,1,0:T(8,128)(2,1)}, u32[]{:S(2)}, u32[]{:S(2)}) async-start(bf16[16,256,2048]{2,1,0:T(8,128)(2,1)} %bitcast.113), calls=%async_computation.2 | async-start | bytes 33554432 | tf_op jit(solution)/shard_map/all_to_all | solution.py:146
  658.8 829.2 %all-gather.11.cloned.1.call-start = ((), (), s32[]{:S(2)}) async-start(), calls=%async_computation.12 | async-start | bytes 18874368 | tf_op jit(solution)/shard_map/all_gather | solution.py:118
  841.9 190.6 %all-to-all-start = ((bf16[16,256,2048]{2,1,0:T(8,128)(2,1)}), bf16[16,256,2048]{2,1,0:T(8,128)(2,1)}, u32[]{:S(2)}, u32[]{:S(2)}) async-start(bf16[16,256,2048]{2,1,0:T(8,128)(2,1)} %bitcast.112), calls=%async_computation | async-start | bytes 33554432 | tf_op jit(solution)/shard_map/all_to_all | solution.py:109
  1574.3 190.1 %all-to-all-start.1 = ((bf16[4,1024,2048]{2,0,1:T(4,128)(2,1)}), bf16[4,1024,2048]{2,0,1:T(4,128)(2,1)}, u32[]{:S(2)}, u32[]{:S(2)}) async-start(bf16[4,1024,2048]{2,0,1:T(4,128)(2,1)} %copy.196), calls=%async_computation.1 | async-start | bytes 33554432 | tf_op jit(solution)/shard_map/all_to_all | solution.py:130
  1646.9 124.8 %copy-start.58 = (s32[2048,1]{0,1:T(1,128)S(1)}, s32[2048,1]{0,1:T(1,128)}, u32[]{:S(2)}) copy-start(s32[2048,1]{0,1:T(1,128)} %copy-done.57) | copy-start | bytes 24580
  1764.5 190.3 %all-to-all-start.3 = ((bf16[4,1024,2048]{2,0,1:T(4,128)(2,1)}), bf16[4,1024,2048]{2,0,1:T(4,128)(2,1)}, u32[]{:S(2)}, u32[]{:S(2)}) async-start(bf16[4,1024,2048]{2,0,1:T(4,128)(2,1)} %copy.202), calls=%async_computation.3 | async-start | bytes 33554432 | tf_op jit(solution)/shard_map/all_to_all | solution.py:172
  1771.7 396.0 %reduce-scatter.8.cloned.1.call-start = ((), (), s32[]{:S(2)}) async-start(), calls=%async_computation.14 | async-start | bytes 9437184 | tf_op jit(solution)/shard_map/reduce_scatter | solution.py:245
  1790.4 24.4 copy-start.11
  1790.4 24.4 copy-start.33
  1814.8 9.6 copy-start.41
  1814.8 9.6 copy-start.60
  1814.8 9.6 copy-start.64
  1814.8 9.6 copy-start.55
  1998.0 11.4 copy-start.3
  1998.0 11.4 copy-start.37
  1998.0 11.4 copy-start.53
  1998.0 11.4 copy-start.62
  2009.4 3.1 copy-start.25
  2009.4 3.1 copy-start.27
  2012.6 3.1 copy-start.19
  2021.3 553.5 %reduce-scatter.6.cloned.1.call-start = ((), (), s32[]{:S(2)}) async-start(), calls=%async_computation.13 | async-start | bytes 28311552 | tf_op jit(solution)/shard_map/reduce_scatter | solution.py:242
  2029.5 4.1 copy-start.1
  2036.9 2.2 copy-start.6
  2036.9 2.2 copy-start.38
  2036.9 2.2 copy-start.45
  2036.9 2.2 copy-start.47
  2036.9 2.2 copy-start.68
  2036.9 2.2 copy-start.70
  2039.1 3.0 copy-start.13
  2042.9 2.1 copy-start.15
  2059.8 620.5 %reduce-scatter.10.cloned.1.call-start = ((), (), s32[]{:S(2)}) async-start(), calls=%async_computation.15 | async-start | bytes 73728 | tf_op jit(solution)/shard_map/reduce_scatter | solution.py:248
  2061.8 856.2 %reduce-scatter.14.cloned.1.call-start = ((), (), s32[]{:S(2)}) async-start(), calls=%async_computation.17 | async-start | bytes 18874368 | tf_op jit(solution)/shard_map/reduce_scatter | solution.py:179
  2089.1 916.2 %all-reduce.4.cloned.1.call-start = ((), (), s32[]{:S(2)}) async-start(), calls=%async_computation.18 | async-start | bytes 8388608 | tf_op jit(solution)/shard_map/psum | solution.py:253
  2574.8 977.9 %reduce-scatter.12.cloned.1.call-start = ((), (), s32[]{:S(2)}) async-start(), calls=%async_computation.16 | async-start | bytes 37748736 | tf_op jit(solution)/shard_map/reduce_scatter | solution.py:176
  2618.7 14.3 copy-start.56
  2618.7 14.3 copy-start.71
  2618.7 14.3 copy-start.72
  2618.7 58.1 %copy-start.9 = (f32[256,2048]{1,0:T(8,128)S(1)}, f32[256,2048]{1,0:T(8,128)}, u32[]{:S(2)}) copy-start(f32[256,2048]{1,0:T(8,128)} %copy-done.7) | copy-start | bytes 6291460
  3005.3 2.9 copy-start.31
  (23 other events, 30.5 us)
Sparse Core Ops, SparseCore 0:
  9.5 484.1 all-gather.4
  495.9 124.8 all-gather.6
  622.4 635.9 all-gather.8
  1260.4 227.5 all-gather.10
  2021.4 146.2 reduce-scatter.7
  2171.9 402.7 reduce-scatter.5
  2578.2 52.8 reduce-scatter.9
  2635.3 282.7 reduce-scatter.13
  2920.5 84.6 all-reduce.3
  3009.3 543.2 reduce-scatter.11
where the time goes:
time: 3570 us
  waiting for transfers between devices  2810 us (79%)
  matrix products  293 us (8%)
  local copies, waits for them, and re-layouts  208 us (6%)
  blocking collectives  118 us (3%)
  other arithmetic  87 us (2%)
    reduce_scatter x1, waiting for transfers between devices, local(): lax.psum_scatter(gate_up_grad_full.astype(jnp.bfloat16), 'fsdp', scatter_...  541 us
    all_gather x1, waiting for transfers between devices, local(): lax.all_gather(qkv_weight, 'fsdp', axis=0, tiled=True)  413 us
    reduce_scatter x1, waiting for transfers between devices, local(): lax.psum_scatter(qkv_grad_full.astype(jnp.bfloat16), 'fsdp', scatter_dime...  407 us
    reduce_scatter x1, waiting for transfers between devices, local(): lax.psum_scatter(down_grad_full.astype(jnp.bfloat16), 'fsdp', scatter_dim...  231 us
    all_gather x1, waiting for transfers between devices, local(): lax.all_gather(gate_up_weight, 'fsdp', axis=1, tiled=True)  212 us
    all_gather x1, waiting for transfers between devices, local(): lax.all_gather(down_weight, 'fsdp', axis=1, tiled=True)  187 us
    all_to_all x1, waiting for transfers between devices, local(): lax.all_to_all(outgoing.reshape(experts, capacity, model_width), 'expert'...  169 us
    all_to_all x1, waiting for transfers between devices, local(): lax.all_to_all(grad_out.reshape(experts, capacity, model_width), 'expert'...  161 us
  transfers between devices with their start and end apart: 14, of which 13 were waited for; matrix products, arithmetic and copies ran while one was open for 12% of the time, Pallas kernels for 0%

commit v1 on v0

--- a/solution.py
+++ b/solution.py
@@ -5,6 +5,18 @@
 
 EPSILON = 1e-06
 ROPE_BASE = 50000.0
+
+
+def gather_by_bits(x, axis, dim):
+    ways, here, lap = (lax.axis_size(axis), lax.axis_index(axis), x.shape[dim])
+    line, have = (x, 1)
+    while have < ways:
+        line = jnp.concatenate(
+            [line, lax.ppermute(line, axis, [(d, (d - have) % ways) for d in range(ways)])],
+            axis=dim,
+        )
+        have = 2 * have
+    return jnp.roll(line, here * lap, axis=dim)
 
 
 def normalize(values):
@@ -65,7 +77,7 @@
     unit_one, factor_one = normalize(source)
     normed = (unit_one * attn_gain).astype(jnp.bfloat16)
     qkv_full, out_full, router_full = (
-        lax.all_gather(qkv_weight, "fsdp", axis=0, tiled=True),
+        gather_by_bits(qkv_weight, "fsdp", 0),
         lax.all_gather(out_weight, "fsdp", axis=0, tiled=True),
         lax.all_gather(router_weight, "fsdp", axis=0, tiled=True),
     )

time: 3570 us -> 3840 us (1.076)
  blocking collectives: 118 us -> 912 us
  waiting for transfers between devices: 2810 us -> 2220 us
    all_gather x1, blocking collectives: 67.9 us -> 862 us  [local(): lax.all_gather(router_weight, 'fsdp', axis=0, tiled=True)]
    all_gather x1 -> x0, waiting for transfers between devices: 413 us -> none  [local(): lax.all_gather(qkv_weight, 'fsdp', axis=0, tiled=True)]
    ppermute x0 -> x3, waiting for transfers between devices: none -> 303 us  [gather_by_bits(): lax.ppermute(line, axis, [(d, (d - have) % ways) for d in range(ways)])]
    all_gather x1, waiting for transfers between devices: 212 us -> 0.01 us  [local(): lax.all_gather(gate_up_weight, 'fsdp', axis=1, tiled=True)]
    all_gather x1, waiting for transfers between devices: 187 us -> 0.01 us  [local(): lax.all_gather(down_weight, 'fsdp', axis=1, tiled=True)]
    all_gather x1, waiting for transfers between devices: 83.1 us -> 0.02 us  [local(): lax.all_gather(out_weight, 'fsdp', axis=0, tiled=True)]
  transfers between devices with their start and end apart: 14 -> 16, of which waited for: 13 -> 11; matrix products, arithmetic and copies ran while one was open for 12% -> 12% of each run, Pallas kernels for 0% -> 0%
where the time goes in v1:
time: 3840 us; the launch traced here: 3830 us
  waiting for transfers between devices  2220 us (58%)
  blocking collectives  912 us (24%)
  matrix products  294 us (8%)
  local copies, waits for them, and re-layouts  245 us (6%)
  other arithmetic  97.4 us (3%)
    all_gather x1, blocking collectives, local(): lax.all_gather(router_weight, 'fsdp', axis=0, tiled=True)  862 us
    reduce_scatter x1, waiting for transfers between devices, local(): lax.psum_scatter(gate_up_grad_full.astype(jnp.bfloat16), 'fsdp', scatter_...  541 us
    reduce_scatter x1, waiting for transfers between devices, local(): lax.psum_scatter(qkv_grad_full.astype(jnp.bfloat16), 'fsdp', scatter_dime...  407 us
    ppermute x3, waiting for transfers between devices, gather_by_bits(): lax.ppermute(line, axis, [(d, (d - have) % ways) for d in range(ways)])  303 us
    reduce_scatter x1, waiting for transfers between devices, local(): lax.psum_scatter(down_grad_full.astype(jnp.bfloat16), 'fsdp', scatter_dim...  230 us
    all_to_all x1, waiting for transfers between devices, local(): lax.all_to_all(outgoing.reshape(experts, capacity, model_width), 'expert'...  169 us
    all_to_all x1, waiting for transfers between devices, local(): lax.all_to_all(grad_out.reshape(experts, capacity, model_width), 'expert'...  161 us
    all_to_all x1, waiting for transfers between devices, local(): lax.all_to_all(input_rows, 'expert', split_axis=1, concat_axis=0, tiled=T...  130 us
  transfers between devices with their start and end apart: 16, of which 11 were waited for; matrix products, arithmetic and copies ran while one was open for 12% of the time, Pallas kernels for 0%

profile of v1, /device:TPU:0, one launch (start us, length us, event | category | flops | bytes accessed | tf_op | source)
XLA Modules:
  0.0 3825.9 jit_solution(5520466124504975319)
XLA Ops:
  9.1 6.0 collective-permute-start
  15.0 122.3 %collective-permute-done = bf16[256,6144]{1,0:T(8,128)(2,1)S(1)} collective-permute-done((bf16[256,6144]{1,0:T(8,128)(2,1)S(1)}, bf16[256,6144]{1,0:T(8,128)(2,1)S(1)}, u32[]{:S(2)}, u32[]{:S(2)}) %collective-permute-start) | collective-permute-done | bytes 3145760 | tf_op jit(solution)/shard_map/ppermute | solution.py:15
  138.0 180.4 %collective-permute-done.1 = bf16[512,6144]{1,0:T(8,128)(2,1)S(1)} collective-permute-done((bf16[512,6144]{1,0:T(8,128)(2,1)S(1)}, bf16[512,6144]{1,0:T(8,128)(2,1)S(1)}, u32[]{:S(2)}, u32[]{:S(2)}) %collective-permute-start.1) | collective-permute-done | bytes 6291488 | tf_op jit(solution)/shard_map/ppermute | solution.py:15
  318.4 7.0 pad_maximum_fusion.1
  327.2 2.9 convert_element_type.132
  330.1 861.8 %all_gather.15 = bf16[2048,16]{0,1:T(8,128)(2,1)S(1)} all-gather(bf16[256,16]{0,1:T(8,128)(2,1)S(1)} %copy-done.69), channel_id=1, replica_groups=mesh['expert'=4,'fsdp'=8] {'fsdp'}, dimensions={0}, use_global_device_ids=true | all-gather | bytes 73728 | tf_op jit(solution)/shard_map/all_gather | solution.py:82
  1198.7 3.1 constant_dynamic-update-slice_fusion.5
  1201.7 10.9 constant_dynamic-update-slice_fusion.4
  1216.3 3.1 constant_dynamic-update-slice_fusion.1
  1219.5 10.8 constant_dynamic-update-slice_fusion
  1230.3 11.7 fusion.2
  1242.0 2.2 slice_bitcast_fusion
  1249.0 3.6 multiply_reduce_fusion.9
  1253.6 3.3 copy.225
  1256.9 3.4 copy.186
  1260.3 2.9 multiply_reduce_fusion.10
  1264.3 2.2 multiply_multiply_fusion
  1272.1 2.1 convolution_convert_fusion.9
  1275.2 5.8 multiply_reduce_fusion.8
  1284.0 22.2 scatter_custom_fusion.1
  1306.2 7.0 all-to-all-start.2
  1314.0 21.5 scatter_custom_fusion
  1335.4 160.8 %all-to-all-done.2 = bf16[16,256,2048]{2,1,0:T(8,128)(2,1)} async-done(((bf16[16,256,2048]{2,1,0:T(8,128)(2,1)}), bf16[16,256,2048]{2,1,0:T(8,128)(2,1)}, u32[]{:S(2)}, u32[]{:S(2)}) %all-to-all-start.2) | async-done | bytes 16777248 | tf_op jit(solution)/shard_map/all_to_all | solution.py:158
  1496.3 7.8 all-to-all-start
  1504.1 14.1 copy.199
  1518.2 168.9 %all-to-all-done = bf16[16,256,2048]{2,1,0:T(8,128)(2,1)} async-done(((bf16[16,256,2048]{2,1,0:T(8,128)(2,1)}), bf16[16,256,2048]{2,1,0:T(8,128)(2,1)}, u32[]{:S(2)}, u32[]{:S(2)}) %all-to-all-start) | async-done | bytes 16777248 | tf_op jit(solution)/shard_map/all_to_all | solution.py:121
  1687.1 14.1 copy.195
  1701.3 43.2 %fusion.57 = f32[4,1024,2048]{2,1,0:T(8,128)} fusion(bf16[4,1024,2048]{2,1,0:T(8,128)(2,1)} %bitcast.118, bf16[4,2048,2048]{2,1,0:T(8,128)(2,1)} %all-gather.6.cloned.1.call-done), kind=kOutput, calls=%fused_computation.152 | convolution fusion | flops 34359738368 | bytes 83886080 | tf_op jit(solution)/shard_map/erd,edf->erf/dot_general | solution.py:132
  1744.4 37.0 multiply_convert_fusion.1
  1781.4 27.3 convolution_convert_fusion.4
  1808.8 22.1 copy.196
  1830.9 7.0 all-to-all-start.1
  1837.9 43.4 %convolution_convert_fusion.2 = bf16[4,1024,2048]{2,1,0:T(8,128)(2,1)} fusion(bf16[4,2048,2048]{2,1,0:T(8,128)(2,1)} %all-gather.6.cloned.1.call-done, bf16[4,1024,1024]{2,1,0:T(8,128)(2,1)} %get-tuple-element.30, bf16[4,1024,1024]{2,1,0:T(8,128)(2,1)} %get-tuple-element.29), kind=kOutput, calls=%fused_computation.22 | convolution fusion | flops 34401681408 | bytes 67108864 | tf_op jit(solution)/shard_map/erf,edf->erd/dot_general | solution.py:181
  1881.3 22.1 copy.202
  1903.5 117.5 %all-to-all-done.1 = bf16[4,1024,2048]{2,0,1:T(4,128)(2,1)} async-done(((bf16[4,1024,2048]{2,0,1:T(4,128)(2,1)}), bf16[4,1024,2048]{2,0,1:T(4,128)(2,1)}, u32[]{:S(2)}, u32[]{:S(2)}) %all-to-all-start.1) | async-done | bytes 16777248 | tf_op jit(solution)/shard_map/all_to_all | solution.py:142
  2021.0 7.2 all-to-all-start.3
  2028.3 18.7 copy.197
  2046.9 24.4 gather_fusion
  2071.4 9.5 fusion.5
  2081.1 130.2 %all-to-all-done.3 = bf16[4,1024,2048]{2,0,1:T(4,128)(2,1)} async-done(((bf16[4,1024,2048]{2,0,1:T(4,128)(2,1)}), bf16[4,1024,2048]{2,0,1:T(4,128)(2,1)}, u32[]{:S(2)}, u32[]{:S(2)}) %all-to-all-start.3) | async-done | bytes 16777248 | tf_op jit(solution)/shard_map/all_to_all | solution.py:184
  2211.2 18.7 copy.203
  2229.9 24.7 gather_fusion.1
  2254.6 11.5 convert_reduce_fusion
  2266.1 3.1 multiply_reduce_fusion.2
  2272.4 5.7 convolution_convert_fusion.5
  2279.7 5.8 convolution_convert_fusion.6
  2286.0 4.1 multiply_reduce_fusion
  2295.6 3.0 multiply_reduce_fusion.4
  2301.6 14.7 convolution_convert_fusion.1
  2318.5 27.4 convolution_convert_fusion.3
  2346.0 81.7 %reduce-scatter.8.cloned.1.call-done = bf16[256,2048]{1,0:T(8,128)(2,1)} async-done(((bf16[2048,2048]{1,0:T(8,128)(2,1)}), bf16[256,2048]{1,0:T(8,128)(2,1)}) %reduce-scatter.8.cloned.1.call-update) | async-done | bytes 1048592 | tf_op jit(solution)/shard_map/reduce_scatter | solution.py:257
  2427.7 406.9 %reduce-scatter.6.cloned.1.call-done = bf16[256,6144]{1,0:T(8,128)(2,1)} async-done(((bf16[2048,6144]{1,0:T(8,128)(2,1)}), bf16[256,6144]{1,0:T(8,128)(2,1)}) %reduce-scatter.6.cloned.1.call-update) | async-done | bytes 3145744 | tf_op jit(solution)/shard_map/reduce_scatter | solution.py:254
  2834.6 43.8 %convolution_convert_fusion = bf16[4,2048,2048]{2,1,0:T(8,128)(2,1)} fusion(bf16[4,1024,2048]{2,1,0:T(8,128)(2,1)} %bitcast.119, bf16[4,1024,1024]{2,1,0:T(8,128)(2,1)} %get-tuple-element.30, bf16[4,1024,1024]{2,1,0:T(8,128)(2,1)} %get-tuple-element.29), kind=kOutput, calls=%fused_computation.4 | convolution fusion | flops 34410070016 | bytes 67108864 | tf_op jit(solution)/shard_map/erd,erf->edf/dot_general | solution.py:178
  2878.6 14.2 fusion.26
  2892.8 43.8 %all-reduce = (f32[2048]{0:T(1024)}, f32[128]{0:T(128)}, f32[128]{0:T(128)}, f32[2048]{0:T(1024)}) all-reduce(f32[2048]{0:T(1024)S(1)} %get-tuple-element.19, f32[128]{0:T(128)S(1)} %copy-done.74, f32[128]{0:T(128)S(1)} %copy-done.75, f32[2048]{0:T(1024)S(1)} %copy-done.59), channel_id=1, replica_groups=mesh['expert'=4,'fsdp'=8] {'expert','fsdp'}, use_global_device_ids=true, to_apply=%region_22.23 | all-reduce | flops 4352 | bytes 34816 | tf_op jit(solution)/shard_map/psum | solution.py:269
  2936.6 3.5 fusion.25
  2940.1 6.7 psum.55
  2947.5 230.1 %reduce-scatter.14.cloned.1.call-done = bf16[4,128,2048]{2,1,0:T(8,128)(2,1)} async-done(((bf16[4,1024,2048]{2,1,0:T(8,128)(2,1)}), bf16[4,128,2048]{2,1,0:T(8,128)(2,1)}) %reduce-scatter.14.cloned.1.call-update) | async-done | bytes 2097168 | tf_op jit(solution)/shard_map/reduce_scatter | solution.py:191
  3177.6 4.1 convert_element_type.150
  3181.8 83.1 %all-reduce.4.cloned.1.call-done = (bf16[256,6144]{1,0:T(8,128)(2,1)}, bf16[256,2048]{1,0:T(8,128)(2,1)}) async-done(((bf16[256,6144]{1,0:T(8,128)(2,1)}, bf16[256,2048]{1,0:T(8,128)(2,1)}), (bf16[256,6144]{1,0:T(8,128)(2,1)}, bf16[256,2048]{1,0:T(8,128)(2,1)})) %all-reduce.4.cloned.1.call-update) | async-done | bytes 4194320 | tf_op jit(solution)/shard_map/psum | solution.py:265
  3264.8 2.9 convert_element_type.144
  3267.8 3.4 convert_element_type.142
  3271.2 541.1 %reduce-scatter.12.cloned.1.call-done = bf16[4,256,2048]{2,1,0:T(8,128)(2,1)} async-done(((bf16[4,2048,2048]{2,1,0:T(8,128)(2,1)}), bf16[4,256,2048]{2,1,0:T(8,128)(2,1)}) %reduce-scatter.12.cloned.1.call-update) | async-done | bytes 4194320 | tf_op jit(solution)/shard_map/reduce_scatter | solution.py:188
  3812.3 6.7 convert_element_type.148
  (239 shorter events, 48.2 us)
Async XLA Ops:
  7.2 1267.1 %all-gather.4.cloned.1.call-start = ((), (), s32[]{:S(2)}) async-start(), calls=%async_computation.9 | async-start | bytes 9437184 | tf_op jit(solution)/shard_map/all_gather | solution.py:81
  7.9 1693.3 %all-gather.6.cloned.1.call-start = ((), (), s32[]{:S(2)}) async-start(), calls=%async_computation.10 | async-start | bytes 37748736 | tf_op jit(solution)/shard_map/all_gather | solution.py:129
  9.1 128.3 %collective-permute-start = (bf16[256,6144]{1,0:T(8,128)(2,1)S(1)}, bf16[256,6144]{1,0:T(8,128)(2,1)S(1)}, u32[]{:S(2)}, u32[]{:S(2)}) collective-permute-start(bf16[256,6144]{1,0:T(8,128)(2,1)S(1)} %copy-done.3), channel_id=1, source_target_pairs={{0,7},{1,0},{2,1},{3,2},{4,3},{5,4},{6,5},{7,6},{8,15},{9,8},{10,9... | collective-permute-start | bytes 9437192 | tf_op jit(solution)/shard_map/ppermute | solution.py:15
  137.3 181.1 %copy-start.4 = (bf16[256,6144]{1,0:T(8,128)(2,1)}, bf16[256,6144]{1,0:T(8,128)(2,1)S(1)}, u32[]{:S(2)}) copy-start(bf16[256,6144]{1,0:T(8,128)(2,1)S(1)} %collective-permute-done) | copy-start | bytes 9437188
  137.9 189.0 %copy-start.57 = (s32[256,8]{0,1:T(8,128)S(1)}, s32[256,8]{0,1:T(8,128)}, u32[]{:S(2)}) copy-start(s32[256,8]{0,1:T(8,128)} %param.14) | copy-start | bytes 24580
  137.9 189.0 %copy-start.68 = (s32[256,8]{0,1:T(8,128)S(1)}, s32[256,8]{0,1:T(8,128)}, u32[]{:S(2)}) copy-start(s32[256,8]{0,1:T(8,128)} %param.15) | copy-start | bytes 24580
  137.9 192.1 %copy-start.69 = (bf16[256,16]{0,1:T(8,128)(2,1)S(1)}, bf16[256,16]{0,1:T(8,128)(2,1)}, u32[]{:S(2)}) copy-start(bf16[256,16]{0,1:T(8,128)(2,1)} %param.22) | copy-start | bytes 24580
  138.0 180.4 %collective-permute-start.1 = (bf16[512,6144]{1,0:T(8,128)(2,1)S(1)}, bf16[512,6144]{1,0:T(8,128)(2,1)S(1)}, u32[]{:S(2)}, u32[]{:S(2)}) collective-permute-start(bf16[512,6144]{1,0:T(8,128)(2,1)S(1)} %pad_maximum_fusion.4), channel_id=1, source_target_pairs={{0,6},{1,7},{2,0},{3,1},{4,2},{5,3},{6,4},{7,5},{8,14},{9,15},{10,... | collective-permute-start | bytes 18874376 | tf_op jit(solution)/shard_map/ppermute | solution.py:15
  318.4 7.0 copy-start.2
  325.4 876.4 %collective-permute-start.2 = (bf16[1024,6144]{1,0:T(8,128)(2,1)}, bf16[1024,6144]{1,0:T(8,128)(2,1)}, u32[]{:S(2)}, u32[]{:S(2)}) collective-permute-start(bf16[1024,6144]{1,0:T(8,128)(2,1)} %pad_maximum_fusion.1), channel_id=1, source_target_pairs={{0,4},{1,5},{2,6},{3,7},{4,0},{5,1},{6,2},{7,3},{8,12},{9,13},{10,... | collective-permute-start | bytes 37748744 | tf_op jit(solution)/shard_map/ppermute | solution.py:15
  330.1 866.7 %copy-start.5 = (bf16[256,6144]{1,0:T(8,128)(2,1)S(1)}, bf16[256,6144]{1,0:T(8,128)(2,1)}, u32[]{:S(2)}) copy-start(bf16[256,6144]{1,0:T(8,128)(2,1)} %copy-done.4) | copy-start | bytes 9437188
  1191.9 90.8 %copy-start.39 = (bf16[2048,16]{0,1:T(8,128)(2,1)}, bf16[2048,16]{0,1:T(8,128)(2,1)S(1)}, u32[]{:S(2)}) copy-start(bf16[2048,16]{0,1:T(8,128)(2,1)S(1)} %all_gather.15) | copy-start | bytes 196612
  1193.2 5.5 slice-start
  1194.8 35.4 copy-start.53
  1194.9 119.1 %copy-start.60 = (s32[2048,1]{0,1:T(1,128)}, s32[2048,1]{0,1:T(1,128)S(1)}, u32[]{:S(2)}) copy-start(s32[2048,1]{0,1:T(1,128)S(1)} %compare_select_fusion) | copy-start | bytes 24580
  1194.9 3.8 slice-start.1
  1219.4 10.8 copy-start.18
  1219.5 10.8 copy-start.37
  1242.0 3.3 copy-start.24
  1249.0 15.2 copy-start.8
  1256.9 7.3 copy-start.70
  1256.9 7.3 copy-start.72
  1264.2 2.3 copy-start.47
  1264.2 2.2 copy-start.49
  1275.2 7.2 copy-start.55
  1281.1 2.9 copy-start.14
  1281.1 25.1 copy-start.64
  1282.7 31.3 copy-start.20
  1283.7 22.5 copy-start.66
  1283.9 22.3 copy-start.35
  1306.2 190.1 %all-to-all-start.2 = ((bf16[16,256,2048]{2,1,0:T(8,128)(2,1)}), bf16[16,256,2048]{2,1,0:T(8,128)(2,1)}, u32[]{:S(2)}, u32[]{:S(2)}) async-start(bf16[16,256,2048]{2,1,0:T(8,128)(2,1)} %bitcast.111), calls=%async_computation.2 | async-start | bytes 33554432 | tf_op jit(solution)/shard_map/all_to_all | solution.py:158
  1313.2 431.2 %all-gather.8.cloned.1.call-start = ((), (), s32[]{:S(2)}) async-start(), calls=%async_computation.11 | async-start | bytes 18874368 | tf_op jit(solution)/shard_map/all_gather | solution.py:130
  1496.3 190.9 %all-to-all-start = ((bf16[16,256,2048]{2,1,0:T(8,128)(2,1)}), bf16[16,256,2048]{2,1,0:T(8,128)(2,1)}, u32[]{:S(2)}, u32[]{:S(2)}) async-start(bf16[16,256,2048]{2,1,0:T(8,128)(2,1)} %bitcast.110), calls=%async_computation | async-start | bytes 33554432 | tf_op jit(solution)/shard_map/all_to_all | solution.py:121
  1830.9 190.1 %all-to-all-start.1 = ((bf16[4,1024,2048]{2,0,1:T(4,128)(2,1)}), bf16[4,1024,2048]{2,0,1:T(4,128)(2,1)}, u32[]{:S(2)}, u32[]{:S(2)}) async-start(bf16[4,1024,2048]{2,0,1:T(4,128)(2,1)} %copy.196), calls=%async_computation.1 | async-start | bytes 33554432 | tf_op jit(solution)/shard_map/all_to_all | solution.py:142
  1903.5 124.8 %copy-start.61 = (s32[2048,1]{0,1:T(1,128)S(1)}, s32[2048,1]{0,1:T(1,128)}, u32[]{:S(2)}) copy-start(s32[2048,1]{0,1:T(1,128)} %copy-done.60) | copy-start | bytes 24580
  2021.0 190.3 %all-to-all-start.3 = ((bf16[4,1024,2048]{2,0,1:T(4,128)(2,1)}), bf16[4,1024,2048]{2,0,1:T(4,128)(2,1)}, u32[]{:S(2)}, u32[]{:S(2)}) async-start(bf16[4,1024,2048]{2,0,1:T(4,128)(2,1)} %copy.202), calls=%async_computation.3 | async-start | bytes 33554432 | tf_op jit(solution)/shard_map/all_to_all | solution.py:184
  2028.2 399.5 %reduce-scatter.8.cloned.1.call-start = ((), (), s32[]{:S(2)}) async-start(), calls=%async_computation.13 | async-start | bytes 9437184 | tf_op jit(solution)/shard_map/reduce_scatter | solution.py:257
  2046.9 24.4 copy-start.15
  2046.9 24.4 copy-start.36
  2071.3 9.6 copy-start.44
  2071.3 9.6 copy-start.63
  2071.4 9.6 copy-start.67
  2071.4 9.7 copy-start.58
  2254.6 11.5 copy-start.7
  2254.6 11.5 copy-start.40
  2254.6 11.5 copy-start.56
  2254.6 11.5 copy-start.65
  2266.1 3.1 copy-start.29
  2266.1 3.1 copy-start.30
  2269.3 3.1 copy-start.23
  2278.1 556.5 %reduce-scatter.6.cloned.1.call-start = ((), (), s32[]{:S(2)}) async-start(), calls=%async_computation.12 | async-start | bytes 28311552 | tf_op jit(solution)/shard_map/reduce_scatter | solution.py:254
  2286.0 4.1 copy-start.1
  2293.3 2.2 copy-start.10
  2293.3 2.2 copy-start.41
  2295.6 3.0 copy-start.17
  2316.3 623.8 %reduce-scatter.10.cloned.1.call-start = ((), (), s32[]{:S(2)}) async-start(), calls=%async_computation.14 | async-start | bytes 73728 | tf_op jit(solution)/shard_map/reduce_scatter | solution.py:260
  2318.4 859.2 %reduce-scatter.14.cloned.1.call-start = ((), (), s32[]{:S(2)}) async-start(), calls=%async_computation.16 | async-start | bytes 18874368 | tf_op jit(solution)/shard_map/reduce_scatter | solution.py:191
  2345.9 918.9 %all-reduce.4.cloned.1.call-start = ((), (), s32[]{:S(2)}) async-start(), calls=%async_computation.17 | async-start | bytes 8388608 | tf_op jit(solution)/shard_map/psum | solution.py:265
  2834.6 977.7 %reduce-scatter.12.cloned.1.call-start = ((), (), s32[]{:S(2)}) async-start(), calls=%async_computation.15 | async-start | bytes 37748736 | tf_op jit(solution)/shard_map/reduce_scatter | solution.py:188
  2878.5 14.3 copy-start.59
  2878.5 14.3 copy-start.74
  2878.5 14.3 copy-start.75
  2878.5 58.1 %copy-start.13 = (f32[256,2048]{1,0:T(8,128)S(1)}, f32[256,2048]{1,0:T(8,128)}, u32[]{:S(2)}) copy-start(f32[256,2048]{1,0:T(8,128)} %copy-done.11) | copy-start | bytes 6291460
  3264.8 2.9 copy-start.34
  (30 other events, 44.4 us)
Sparse Core Ops, SparseCore 0:
  10.1 220.7 all-gather.3
  232.4 788.8 all-gather.5
  1316.2 229.7 all-gather.7
  2278.2 149.4 reduce-scatter.7
  2431.9 402.6 reduce-scatter.5
  2837.9 52.7 reduce-scatter.9
  2894.9 282.6 reduce-scatter.13
  3180.0 84.7 all-reduce.3
  3269.1 543.1 reduce-scatter.11
